TPU v7x, 32 devices: a whole 2x2x4 slice. The times are simulated.
32 devices in a mesh: dp: 4 (over y, core), expert: 8 (over z, x).
Axes of the slice: x: 2, y: 2, z: 4, core: 2. Of those that a mesh axis runs over, the one named last changes fastest.
Arguments:
- hidden_in: bfloat16 [2048, 2048], P(('dp', 'expert')), may hold values from -6 to 6
- context: bfloat16 [2048, 2048], P(('dp', 'expert')), may hold values from -6 to 6
- out_proj: bfloat16 [2048, 2048], P(('dp', 'expert')), may hold values from -0.125 to 0.125
- norm_gain: float32 [2048], replicated, may hold values from 0.5 to 1.5
- router: bfloat16 [2048, 64], P(('dp', 'expert')), may hold values from -0.25 to 0.25
- expert_ids: int32 [2048, 8], P(('dp', 'expert')), may hold values from 0 to 63, as said below
- replica_expert: int32 [128], replicated, may hold values from 0 to 63, as said below
- split_pick: int32 [2048, 8], P(('dp', 'expert')), may hold values from 0 to 65535
- up_gate: bfloat16 [128, 2048, 2048], P(('dp', 'expert')), may hold values from -0.125 to 0.125
- down: bfloat16 [128, 1024, 2048], P(('dp', 'expert')), may hold values from -0.1875 to 0.1875
Outputs:
- layer_out: bfloat16 [2048, 2048], P(('dp', 'expert'))
Inputs may be any that keep to these rules, and one draw needn't show every extreme that they name: `expert_ids`: each row names 8 different experts. `replica_expert`: every expert is served by one replica or more.
All inputs are finite; a program needn't handle non-finite values.
Results may differ from a plain program's by a relative error of at most 0.004.
Values may be sent and summed in bfloat16 or wider, within the bound.
A program may use at most 128 MiB of HBM per device.

v0:
```python
import jax
import jax.numpy as jnp
from jax import lax
from jax.sharding import PartitionSpec as P


def rms_norm(residual, norm_gain):
    scale_back = lax.rsqrt(jnp.mean(residual * residual, axis=-1, keepdims=True) + 1e-05)
    return (residual * scale_back * norm_gain).astype(jnp.bfloat16)


def route_block(expert_ids, split_pick, replica_expert):
    replica_total = replica_expert.shape[0]
    replica_iota = lax.iota(jnp.int32, replica_total)
    same_expert = replica_expert[:, None] == replica_expert[None, :]
    earlier = replica_iota[:, None] > replica_iota[None, :]
    replica_rank = jnp.sum((same_expert & earlier).astype(jnp.int32), axis=1)
    serves = expert_ids[:, :, None] == replica_expert[None, None, :]
    replica_count = jnp.sum(serves.astype(jnp.int32), axis=-1)
    wanted = split_pick % replica_count
    matches = serves & (replica_rank[None, None, :] == wanted[:, :, None])
    replica = jnp.sum(jnp.where(matches, replica_iota[None, None, :], 0), axis=-1)
    flat_replica = replica.reshape(-1)
    pair_iota = lax.iota(jnp.int32, flat_replica.shape[0])
    same_target = flat_replica[:, None] == flat_replica[None, :]
    before = pair_iota[:, None] > pair_iota[None, :]
    slot_index = jnp.sum((same_target & before).astype(jnp.int32), axis=1)
    return (replica, slot_index.reshape(replica.shape))


def apply_experts(incoming, up_gate, down, capacity):
    arrived_shape = incoming.shape
    local_reps = up_gate.shape[0]
    hidden_units = down.shape[1]
    stacked = incoming.reshape(-1, local_reps, capacity, incoming.shape[-1])
    gate_up = jnp.einsum("sjcd,jdf->sjcf", stacked, up_gate, preferred_element_type=jnp.float32)
    hidden_act = (jax.nn.silu(gate_up[..., :hidden_units]) * gate_up[..., hidden_units:]).astype(
        jnp.bfloat16
    )
    expert_out = jnp.einsum("sjcf,jfd->sjcd", hidden_act, down, preferred_element_type=jnp.float32)
    return expert_out.astype(jnp.bfloat16).reshape(arrived_shape)


def per_device(
    hidden_in,
    context,
    out_proj,
    norm_gain,
    router,
    expert_ids,
    replica_expert,
    split_pick,
    up_gate,
    down,
):
    tok_rows, model_width = hidden_in.shape
    top_count = expert_ids.shape[1]
    replica_total = replica_expert.shape[0]
    local_reps = up_gate.shape[0]
    data_groups = lax.axis_size("dp")
    expert_groups = lax.axis_size("expert")
    capacity = max(2, 2 * tok_rows * top_count // replica_total)
    summed = jnp.dot(
        context,
        lax.all_gather(out_proj, ("dp", "expert"), axis=0, tiled=True),
        preferred_element_type=jnp.float32,
    )
    router_rows = lax.all_gather(router, ("dp", "expert"), axis=0, tiled=True)
    residual = hidden_in.astype(jnp.float32) + summed
    normed = rms_norm(residual, norm_gain)
    logits = jnp.dot(normed, router_rows, preferred_element_type=jnp.float32)
    hit_mask = expert_ids[:, :, None] == lax.iota(jnp.int32, logits.shape[1])[None, None, :]
    chosen = jnp.sum(jnp.where(hit_mask, logits[:, None, :], 0.0), axis=-1)
    raised = jnp.exp(chosen)
    route_weight = raised / jnp.sum(raised, axis=-1, keepdims=True)
    replica, slot_index = route_block(expert_ids, split_pick, replica_expert)
    within_cap = slot_index < capacity
    buffer_row = jnp.where(within_cap, replica * capacity + slot_index, -1).reshape(-1)
    slot_total = replica_total * capacity
    matches = buffer_row[None, :] == lax.iota(jnp.int32, slot_total)[:, None]
    filled = jnp.any(matches, axis=1)
    row_of_pair = lax.iota(jnp.int32, tok_rows * top_count) // top_count
    anchor = jnp.sum(jnp.where(matches, row_of_pair[None, :], 0), axis=1)
    outgoing = jnp.where(filled[:, None], normed[anchor], jnp.zeros((), jnp.bfloat16))
    outgoing = outgoing.reshape(data_groups, expert_groups, local_reps * capacity, model_width)
    incoming = lax.all_to_all(
        lax.all_to_all(outgoing, "expert", split_axis=1, concat_axis=1, tiled=True),
        "dp",
        split_axis=0,
        concat_axis=0,
        tiled=True,
    )
    results = apply_experts(incoming, up_gate, down, capacity)
    returned = lax.all_to_all(
        lax.all_to_all(results, "dp", split_axis=0, concat_axis=0, tiled=True),
        "expert",
        split_axis=1,
        concat_axis=1,
        tiled=True,
    )
    returned = returned.reshape(slot_total, model_width)
    safe_index = jnp.where(within_cap, replica * capacity + slot_index, 0)
    gathered = returned[safe_index]
    kept_weight = jnp.where(within_cap, route_weight, 0.0)
    layer_out = residual + jnp.sum(kept_weight[:, :, None] * gathered.astype(jnp.float32), axis=1)
    return layer_out.astype(jnp.bfloat16)


def per_device_gathered(
    hidden_in,
    context,
    out_proj,
    norm_gain,
    router,
    expert_ids,
    replica_expert,
    split_pick,
    up_gate,
    down,
):
    axes = ("dp", "expert")
    tok_rows, model_width = hidden_in.shape
    top_count = expert_ids.shape[1]
    replica_total = replica_expert.shape[0]
    local_reps = up_gate.shape[0]
    hidden_units = down.shape[1]
    blocks = lax.axis_size("dp") * lax.axis_size("expert")
    me = lax.axis_index("dp") * lax.axis_size("expert") + lax.axis_index("expert")
    capacity = max(2, 2 * tok_rows * top_count // replica_total)
    local_slots = local_reps * capacity
    proj_rows = lax.all_gather(out_proj, axes, axis=0, tiled=True)
    router_rows = lax.all_gather(router, axes, axis=0, tiled=True)
    replica, slot_index = route_block(expert_ids, split_pick, replica_expert)
    position = jnp.where(slot_index < capacity, replica * capacity + slot_index, -1)
    positions = lax.all_gather(position, axes, axis=0, tiled=False)
    summed = jnp.dot(context, proj_rows, preferred_element_type=jnp.float32)
    residual = hidden_in.astype(jnp.float32) + summed
    normed = rms_norm(residual, norm_gain)
    all_normed = lax.all_gather(normed, axes, axis=0, tiled=False)
    logits = jnp.dot(normed, router_rows, preferred_element_type=jnp.float32)
    hit_mask = expert_ids[:, :, None] == lax.iota(jnp.int32, logits.shape[1])[None, None, :]
    chosen = jnp.sum(jnp.where(hit_mask, logits[:, None, :], 0.0), axis=-1)
    raised = jnp.exp(chosen)
    route_weight = raised / jnp.sum(raised, axis=-1, keepdims=True)
    weights = lax.all_gather(route_weight, axes, axis=0, tiled=False)
    local_iota = lax.iota(jnp.int32, local_slots)
    hits = (positions - me * local_slots)[:, :, :, None] == local_iota
    pick = jnp.any(hits, axis=2)
    slot_weight = jnp.sum(jnp.where(hits, weights[:, :, :, None], 0.0), axis=2)
    expert_in = jnp.einsum(
        "btjc,btd->jbcd",
        pick.astype(jnp.bfloat16).reshape(blocks, tok_rows, local_reps, capacity),
        all_normed,
        preferred_element_type=jnp.float32,
    ).astype(jnp.bfloat16)
    expert_in = expert_in.reshape(local_reps, blocks * capacity, model_width)
    gate_up = jnp.einsum("jsd,jdf->jsf", expert_in, up_gate, preferred_element_type=jnp.float32)
    hidden_act = (jax.nn.silu(gate_up[..., :hidden_units]) * gate_up[..., hidden_units:]).astype(
        jnp.bfloat16
    )
    expert_out = jnp.einsum("jsf,jfd->jsd", hidden_act, down, preferred_element_type=jnp.float32)
    expert_out = expert_out.astype(jnp.bfloat16).reshape(local_reps, blocks, capacity, model_width)
    upper = slot_weight.astype(jnp.bfloat16)
    lower = (slot_weight - upper.astype(jnp.float32)).astype(jnp.bfloat16)
    split = jnp.stack([upper, lower]).reshape(2, blocks, tok_rows, local_reps, capacity)
    twice = jnp.broadcast_to(expert_out[None], (2,) + expert_out.shape)
    partial = jnp.einsum(
        "hbtjc,hjbcd->btd", split, twice, preferred_element_type=jnp.float32
    ).astype(jnp.bfloat16)
    combined = lax.psum_scatter(partial, axes, scatter_dimension=0, tiled=False)
    return (residual + combined.astype(jnp.float32)).astype(jnp.bfloat16)


def solution(mesh):
    device_count = mesh.shape["dp"] * mesh.shape["expert"]
    plan = per_device_gathered if device_count <= 32 else per_device
    return jax.shard_map(
        plan,
        mesh=mesh,
        in_specs=(
            P(("dp", "expert"), None),
            P(("dp", "expert"), None),
            P(("dp", "expert"), None),
            P(),
            P(("dp", "expert"), None),
            P(("dp", "expert"), None),
            P(),
            P(("dp", "expert"), None),
            P(("dp", "expert"), None, None),
            P(("dp", "expert"), None, None),
        ),
        out_specs=P(("dp", "expert"), None),
        check_vma=False,
    )
```

profile of v0, /device:TPU:0, one launch (start us, length us, event | category | flops | bytes accessed | tf_op | source)
XLA Modules:
  0.0 541.7 jit_solution(15114210386043356406)
XLA Ops:
  6.5 0.7 all-gather.4.cloned.1.call-update
  7.4 83.1 %all-gather.4.cloned.1.call-done = bf16[2048,2048]{1,0:T(8,128)(2,1)} async-done(((bf16[64,2048]{1,0:T(8,128)(2,1)}), bf16[2048,2048]{1,0:T(8,128)(2,1)}) %all-gather.4.cloned.1.call-update) | async-done | bytes 8388624 | tf_op jit(solution)/shard_map/all_gather | solution.py:131
  90.5 5.1 multiply_reduce_fusion
  95.6 0.8 multiply_convert_fusion
  96.7 0.2 convert_reduce_fusion.1
  96.9 1.2 fusion.15
  98.1 0.4 add_select_fusion
  98.5 1.3 select_reduce_fusion.2
  99.9 0.3 convert_reduce_fusion
  100.1 0.1 reshape.126
  100.3 68.0 %all_gather.21 = s32[32,64,8]{1,2,0:T(8,128)S(1)} all-gather(s32[1,64,8]{1,2,0:T(8,128)S(1)} %copy.30), channel_id=1, replica_groups=mesh['dp'=4,'expert'=8] {'dp','expert'}, dimensions={0}, use_global_device_ids=true | all-gather | bytes 67584 | tf_op jit(solution)/shard_map/all_gather | solution.py:135
  168.3 66.4 %all_gather.22 = bf16[2048,64]{1,0:T(8,128)(2,1)S(1)} all-gather(bf16[64,64]{1,0:T(8,128)(2,1)S(1)} %copy-done.2), channel_id=1, replica_groups=mesh['dp'=4,'expert'=8] {'dp','expert'}, dimensions={0}, use_global_device_ids=true | all-gather | bytes 270336 | tf_op jit(solution)/shard_map/all_gather | solution.py:132
  234.7 0.7 fusion.5
  235.3 1.2 fusion.20
  236.5 0.2 select_reduce_fusion.1
  236.7 0.1 exponential_reduce_fusion
  237.0 66.4 %all_gather.23 = f32[32,64,8]{1,2,0:T(8,128)S(1)} all-gather(f32[1,64,8]{1,2,0:T(8,128)S(1)} %copy.32), channel_id=1, replica_groups=mesh['dp'=4,'expert'=8] {'dp','expert'}, dimensions={0}, use_global_device_ids=true | all-gather | bytes 67584 | tf_op jit(solution)/shard_map/all_gather | solution.py:145
  303.4 0.9 select_reduce_fusion
  304.4 6.6 %fusion.6 = bf16[4,32,8,2048]{3,2,0,1:T(8,128)(2,1)} fusion(bf16[32,64,2048]{2,1,0:T(8,128)(2,1)} %bitcast.42, pred[32,64,32]{1,2,0:T(8,128)(4,1)S(1)} %fusion.5), kind=kOutput, calls=%fused_computation.12 | convolution fusion | flops 270532608 | bytes 12648448
  311.0 18.3 %fusion.1 = f32[4,256,2048]{2,1,0:T(8,128)} fusion(bf16[4,2048,2048]{2,1,0:T(8,128)(2,1)} %param.18, bf16[4,32,8,2048]{3,2,0,1:T(8,128)(2,1)} %fusion.6), kind=kOutput, calls=%fused_computation.4 | convolution fusion | flops 8589934592 | bytes 46137344 | tf_op jit(solution)/shard_map/jsd,jdf->jsf/dot_general | solution.py:157
  329.3 15.0 %convert_bitcast_fusion = bf16[4,32,8,2048]{3,2,1,0:T(8,128)(2,1)} fusion(bf16[4,1024,2048]{2,1,0:T(8,128)(2,1)} %param.19, f32[4,256,2048]{2,1,0:T(8,128)} %fusion.1), kind=kOutput, calls=%fused_computation.8 | convolution fusion | flops 4303355904 | bytes 29360128 | tf_op jit(solution)/shard_map/jsf,jfd->jsd/dot_general | solution.py:161
  344.3 6.6 %bitcast_convert_fusion = bf16[32,64,2048]{2,1,0:T(8,128)(2,1)} fusion(bf16[1,32,64,4,8]{2,4,3,1,0:T(8,128)(2,1)S(1)} %get-tuple-element.5, bf16[1,32,64,4,8]{2,4,3,1,0:T(8,128)(2,1)S(1)} %get-tuple-element.6, bf16[4,32,8,2048]{3,2,1,0:T(8,128)(2,1)} %convert_bitcast_fusion), kind=kOutput, calls=%fused_computation | convolution fusion | flops 541196288 | bytes 12845056 | tf_op jit(solution)/shard_map/hbtjc,hjbcd->btd/dot_general | solution.py:167
  350.9 182.6 %reduce-scatter.2.cloned.1.call-done = bf16[1,64,2048]{2,1,0:T(8,128)(2,1)} async-done(((bf16[32,64,2048]{2,1,0:T(8,128)(2,1)}), bf16[1,64,2048]{2,1,0:T(8,128)(2,1)}) %reduce-scatter.2.cloned.1.call-update) | async-done | bytes 262160 | tf_op jit(solution)/shard_map/reduce_scatter | solution.py:170
  533.4 1.7 fusion.13
  (30 shorter events, 0.7 us)
Async XLA Ops:
  6.5 84.0 %copy-start = (bf16[64,2048]{1,0:T(8,128)(2,1)S(1)}, bf16[64,2048]{1,0:T(8,128)(2,1)}, u32[]{:S(2)}) copy-start(bf16[64,2048]{1,0:T(8,128)(2,1)} %param.11) | copy-start | bytes 786436
  6.5 84.0 %all-gather.4.cloned.1.call-start = ((), (), s32[]{:S(2)}) async-start(), calls=%async_computation.1 | async-start | bytes 8650752 | tf_op jit(solution)/shard_map/all_gather | solution.py:131
  7.3 88.3 %copy-start.3 = (f32[2048]{0:T(1024)S(1)}, f32[2048]{0:T(1024)}, u32[]{:S(2)}) copy-start(f32[2048]{0:T(1024)} %param.13) | copy-start | bytes 24580
  7.3 89.2 %copy-start.4 = (s32[64,8]{0,1:T(8,128)S(1)}, s32[64,8]{0,1:T(8,128)}, u32[]{:S(2)}) copy-start(s32[64,8]{0,1:T(8,128)} %param.15) | copy-start | bytes 6148
  7.3 89.3 %copy-start.5 = (s32[64,8]{0,1:T(8,128)S(1)}, s32[64,8]{0,1:T(8,128)}, u32[]{:S(2)}) copy-start(s32[64,8]{0,1:T(8,128)} %param.17) | copy-start | bytes 6148
  7.3 89.4 %copy-start.6 = (s32[128]{0:T(128)S(1)}, s32[128]{0:T(128)}, u32[]{:S(2)}) copy-start(s32[128]{0:T(128)} %param.16) | copy-start | bytes 1540
  7.3 161.0 %copy-start.2 = (bf16[64,64]{1,0:T(8,128)(2,1)S(1)}, bf16[64,64]{1,0:T(8,128)(2,1)}, u32[]{:S(2)}) copy-start(bf16[64,64]{1,0:T(8,128)(2,1)} %param.14) | copy-start | bytes 24580
  7.3 297.1 %all-gather.6.cloned.1.call-start = ((), (), s32[]{:S(2)}) async-start(), calls=%async_computation.3 | async-start | bytes 8650752 | tf_op jit(solution)/shard_map/all_gather | solution.py:139
  96.4 437.0 %reduce-scatter.2.cloned.1.call-start = ((), (), s32[]{:S(2)}) async-start(), calls=%async_computation.2 | async-start | bytes 8650752 | tf_op jit(solution)/shard_map/reduce_scatter | solution.py:170
  350.8 184.3 %copy-start.1 = (bf16[64,2048]{1,0:T(8,128)(2,1)S(1)}, bf16[64,2048]{1,0:T(8,128)(2,1)}, u32[]{:S(2)}) copy-start(bf16[64,2048]{1,0:T(8,128)(2,1)} %param.11) | copy-start | bytes 786436
Sparse Core Ops, SparseCore 0:
  10.3 80.1 all-gather.3
  96.6 77.7 all-gather.5
  351.0 182.3 reduce-scatter.1
where the time goes:
time: 542 us
  waiting for transfers between devices  266 us (49%)
  blocking collectives  201 us (37%)
  matrix products  52.6 us (10%)
  between operations  13.3 us (2%)
  other arithmetic  7.94 us (1%)
    reduce_scatter x1, waiting for transfers between devices, per_device_gathered(): combined = lax.psum_scatter(partial, axes, scatter_dimension=0, tiled=False)  183 us
    all_gather x1, waiting for transfers between devices, per_device_gathered(): proj_rows = lax.all_gather(out_proj, axes, axis=0, tiled=True)  83.1 us
    all_gather x1, blocking collectives, per_device_gathered(): positions = lax.all_gather(position, axes, axis=0, tiled=False)  68 us
    all_gather x1, blocking collectives, per_device_gathered(): weights = lax.all_gather(route_weight, axes, axis=0, tiled=False)  66.4 us
    all_gather x1, blocking collectives, per_device_gathered(): router_rows = lax.all_gather(router, axes, axis=0, tiled=True)  66.4 us
    dot_general x1, matrix products, per_device_gathered(): jnp.einsum('jsd,jdf->jsf', expert_in, up_gate, preferred_element_type=jnp...  18.3 us
    dot_general x1, matrix products, per_device_gathered(): jnp.einsum('jsf,jfd->jsd', hidden_act, down, preferred_element_type=jnp.f...  15 us
  transfers between devices with their start and end apart: 3, of which 2 were waited for; matrix products, arithmetic and copies ran while one was open for 1% of the time, Pallas kernels for 0%

commit v1 on v0

--- a/solution.py
+++ b/solution.py
@@ -2,6 +2,13 @@
 import jax.numpy as jnp
 from jax import lax
 from jax.sharding import PartitionSpec as P
+
+
+def time_shapes(target, chunk, device_axis):
+    mixed_arr = jnp.concatenate([target, chunk], axis=1)
+    return jnp.split(
+        jax.lax.all_gather(mixed_arr, device_axis, axis=0, tiled=True), [target.shape[1]], axis=1
+    )
 
 
 def rms_norm(residual, norm_gain):
@@ -128,8 +135,7 @@
     me = lax.axis_index("dp") * lax.axis_size("expert") + lax.axis_index("expert")
     capacity = max(2, 2 * tok_rows * top_count // replica_total)
     local_slots = local_reps * capacity
-    proj_rows = lax.all_gather(out_proj, axes, axis=0, tiled=True)
-    router_rows = lax.all_gather(router, axes, axis=0, tiled=True)
+    proj_rows, router_rows = time_shapes(out_proj, router, axes)
     replica, slot_index = route_block(expert_ids, split_pick, replica_expert)
     position = jnp.where(slot_index < capacity, replica * capacity + slot_index, -1)
     positions = lax.all_gather(position, axes, axis=0, tiled=False)

time: 542 us -> 476 us (0.88)
  blocking collectives: 201 us -> 132 us
    all_gather x1 -> x0, blocking collectives: 66.4 us -> none  [per_device_gathered(): router_rows = lax.all_gather(router, axes, axis=0, tiled=True)]
  transfers between devices with their start and end apart: 3 -> 3, of which waited for: 2 -> 2; matrix products, arithmetic and copies ran while one was open for 1% -> 2% of each run, Pallas kernels for 0% -> 0%
where the time goes in v1:
time: 476 us
  waiting for transfers between devices  267 us (56%)
  blocking collectives  132 us (28%)
  matrix products  52.8 us (11%)
  between operations  13.3 us (3%)
  other arithmetic  9.69 us (2%)
    reduce_scatter x1, waiting for transfers between devices, per_device_gathered(): combined = lax.psum_scatter(partial, axes, scatter_dimension=0, tiled=False)  183 us
    all_gather x1, waiting for transfers between devices, time_shapes(): jax.lax.all_gather(mixed_arr, device_axis, axis=0, tiled=True)  84.3 us
    all_gather x1, blocking collectives, per_device_gathered(): positions = lax.all_gather(position, axes, axis=0, tiled=False)  67.9 us
    all_gather x1, blocking collectives, per_device_gathered(): weights = lax.all_gather(route_weight, axes, axis=0, tiled=False)  64.2 us
    dot_general x1, matrix products, per_device_gathered(): jnp.einsum('jsd,jdf->jsf', expert_in, up_gate, preferred_element_type=jnp...  18.3 us
    dot_general x1, matrix products, per_device_gathered(): jnp.einsum('jsf,jfd->jsd', hidden_act, down, preferred_element_type=jnp.f...  15 us
  transfers between devices with their start and end apart: 3, of which 2 were waited for; matrix products, arithmetic and copies ran while one was open for 2% of the time, Pallas kernels for 0%

profile of v1, /device:TPU:0, one launch (start us, length us, event | category | flops | bytes accessed | tf_op | source)
XLA Modules:
  0.0 475.9 jit_solution(11589045134433765110)
XLA Ops:
  6.5 1.8 pad_maximum_fusion
  8.4 84.3 %all-gather.4.cloned.1.call-done = bf16[2048,2112]{1,0:T(8,128)(2,1)} async-done(((bf16[64,2112]{1,0:T(8,128)(2,1)}), bf16[2048,2112]{1,0:T(8,128)(2,1)}) %all-gather.4.cloned.1.call-update) | async-done | bytes 8650768 | tf_op jit(solution)/shard_map/all_gather | solution.py:10
  92.8 5.1 %multiply_reduce_fusion = (f32[64]{0:T(128)S(1)}, f32[64,2048]{1,0:T(8,128)S(1)}) fusion(bf16[64,2048]{1,0:T(8,128)(2,1)S(1)} %copy-done, bf16[2048,2112]{1,0:T(8,128)(2,1)} %all-gather.4.cloned.1.call-done, bf16[64,2048]{1,0:T(8,128)(2,1)} %param.10), kind=kOutput, calls=%fused_computation.32 | convolution fusion | flops 537395136 | bytes 9437440 | tf_op jit(solution)/shard_map/dot_general | solution.py:142
  97.9 0.8 multiply_convert_fusion
  98.9 0.2 convert_reduce_fusion.1
  99.1 1.2 fusion.25
  100.4 0.4 add_select_fusion
  100.7 1.3 select_reduce_fusion.2
  102.1 0.1 eq.94
  102.1 0.3 convert_reduce_fusion
  102.4 0.1 reshape.126
  102.6 67.9 %all_gather.18 = s32[32,64,8]{1,2,0:T(8,128)S(1)} all-gather(s32[1,64,8]{1,2,0:T(8,128)S(1)} %copy.30), channel_id=1, replica_groups=mesh['dp'=4,'expert'=8] {'dp','expert'}, dimensions={0}, use_global_device_ids=true | all-gather | bytes 67584 | tf_op jit(solution)/shard_map/all_gather | solution.py:141
  170.5 0.7 fusion.7
  171.2 1.3 fusion.18
  172.5 0.2 select_reduce_fusion.1
  172.8 0.1 exponential_reduce_fusion
  173.0 64.2 %all_gather.19 = f32[32,64,8]{1,2,0:T(8,128)S(1)} all-gather(f32[1,64,8]{1,2,0:T(8,128)S(1)} %copy.32), channel_id=1, replica_groups=mesh['dp'=4,'expert'=8] {'dp','expert'}, dimensions={0}, use_global_device_ids=true | all-gather | bytes 67584 | tf_op jit(solution)/shard_map/all_gather | solution.py:151
  237.3 0.9 select_reduce_fusion
  238.3 6.6 %fusion.8 = bf16[4,32,8,2048]{3,2,0,1:T(8,128)(2,1)} fusion(bf16[32,64,2048]{2,1,0:T(8,128)(2,1)} %bitcast.44, pred[32,64,32]{1,2,0:T(8,128)(4,1)S(1)} %fusion.7), kind=kOutput, calls=%fused_computation.14 | convolution fusion | flops 270532608 | bytes 12648448
  244.8 18.3 %fusion.3 = f32[4,256,2048]{2,1,0:T(8,128)} fusion(bf16[4,2048,2048]{2,1,0:T(8,128)(2,1)} %param.18, bf16[4,32,8,2048]{3,2,0,1:T(8,128)(2,1)} %fusion.8), kind=kOutput, calls=%fused_computation.6 | convolution fusion | flops 8589934592 | bytes 46137344 | tf_op jit(solution)/shard_map/jsd,jdf->jsf/dot_general | solution.py:163
  263.1 15.0 %convert_bitcast_fusion = bf16[4,32,8,2048]{3,2,1,0:T(8,128)(2,1)} fusion(bf16[4,1024,2048]{2,1,0:T(8,128)(2,1)} %param.19, f32[4,256,2048]{2,1,0:T(8,128)} %fusion.3), kind=kOutput, calls=%fused_computation.10 | convolution fusion | flops 4303355904 | bytes 29360128 | tf_op jit(solution)/shard_map/jsf,jfd->jsd/dot_general | solution.py:167
  278.1 6.6 %bitcast_convert_fusion = bf16[32,64,2048]{2,1,0:T(8,128)(2,1)} fusion(bf16[1,32,64,4,8]{2,4,3,1,0:T(8,128)(2,1)S(1)} %get-tuple-element.5, bf16[1,32,64,4,8]{2,4,3,1,0:T(8,128)(2,1)S(1)} %get-tuple-element.6, bf16[4,32,8,2048]{3,2,1,0:T(8,128)(2,1)} %convert_bitcast_fusion), kind=kOutput, calls=%fused_computation | convolution fusion | flops 541196288 | bytes 12845056 | tf_op jit(solution)/shard_map/hbtjc,hjbcd->btd/dot_general | solution.py:173
  284.7 183.0 %reduce-scatter.2.cloned.1.call-done = bf16[1,64,2048]{2,1,0:T(8,128)(2,1)} async-done(((bf16[32,64,2048]{2,1,0:T(8,128)(2,1)}), bf16[1,64,2048]{2,1,0:T(8,128)(2,1)}) %reduce-scatter.2.cloned.1.call-update) | async-done | bytes 262160 | tf_op jit(solution)/shard_map/reduce_scatter | solution.py:176
  467.6 1.7 fusion.23
  (28 shorter events, 0.7 us)
Async XLA Ops:
  6.5 86.2 %copy-start = (bf16[64,2048]{1,0:T(8,128)(2,1)S(1)}, bf16[64,2048]{1,0:T(8,128)(2,1)}, u32[]{:S(2)}) copy-start(bf16[64,2048]{1,0:T(8,128)(2,1)} %param.11) | copy-start | bytes 786436
  6.5 86.2 %all-gather.4.cloned.1.call-start = ((), (), s32[]{:S(2)}) async-start(), calls=%async_computation.1 | async-start | bytes 9191424 | tf_op jit(solution)/shard_map/all_gather | solution.py:10
  8.3 89.5 %copy-start.2 = (f32[2048]{0:T(1024)S(1)}, f32[2048]{0:T(1024)}, u32[]{:S(2)}) copy-start(f32[2048]{0:T(1024)} %param.13) | copy-start | bytes 24580
  8.3 90.4 %copy-start.3 = (s32[64,8]{0,1:T(8,128)S(1)}, s32[64,8]{0,1:T(8,128)}, u32[]{:S(2)}) copy-start(s32[64,8]{0,1:T(8,128)} %param.15) | copy-start | bytes 6148
  8.3 90.5 %copy-start.4 = (s32[64,8]{0,1:T(8,128)S(1)}, s32[64,8]{0,1:T(8,128)}, u32[]{:S(2)}) copy-start(s32[64,8]{0,1:T(8,128)} %param.17) | copy-start | bytes 6148
  8.4 90.6 %copy-start.5 = (s32[128]{0:T(128)S(1)}, s32[128]{0:T(128)}, u32[]{:S(2)}) copy-start(s32[128]{0:T(128)} %param.16) | copy-start | bytes 1540
  8.4 229.9 %all-gather.6.cloned.1.call-start = ((), (), s32[]{:S(2)}) async-start(), calls=%async_computation.3 | async-start | bytes 8650752 | tf_op jit(solution)/shard_map/all_gather | solution.py:145
  98.7 368.9 %reduce-scatter.2.cloned.1.call-start = ((), (), s32[]{:S(2)}) async-start(), calls=%async_computation.2 | async-start | bytes 8650752 | tf_op jit(solution)/shard_map/reduce_scatter | solution.py:176
  284.6 184.7 %copy-start.1 = (bf16[64,2048]{1,0:T(8,128)(2,1)S(1)}, bf16[64,2048]{1,0:T(8,128)(2,1)}, u32[]{:S(2)}) copy-start(bf16[64,2048]{1,0:T(8,128)(2,1)} %param.11) | copy-start | bytes 786436
Sparse Core Ops, SparseCore 0:
  10.3 82.4 all-gather.3
  98.8 77.1 all-gather.5
  284.8 182.7 reduce-scatter.1
